TPU v7x, 32 devices: a whole 2x2x4 slice. The times are simulated.
32 devices in a mesh: dp: 4 (over z), expert: 4 (over y, core), loop: 2 (over x).
Axes of the slice: x: 2, y: 2, z: 4, core: 2. Of those that a mesh axis runs over, the one named last changes fastest.
Arguments:
- x_send: bfloat16 [512, 4096], P(('dp', 'expert', 'loop')), may hold values from -6 to 6
- cot_send: bfloat16 [512, 4096], P(('dp', 'expert', 'loop')), may hold values from -6 to 6
- counts: int32 [32, 4], P(('dp', 'expert', 'loop')), may hold values from 0 to 4, as said below
- w_gate: bfloat16 [4, 4096, 768], P('expert', None, 'loop'), may hold values from -0.09375 to 0.09375
- w_up: bfloat16 [4, 4096, 768], P('expert', None, 'loop'), may hold values from -0.09375 to 0.09375
- w_down: bfloat16 [4, 4096, 768], P('expert', None, 'loop'), may hold values from -0.21875 to 0.21875
Outputs:
- grad_rows: bfloat16 [512, 4096], P(('dp', 'expert', 'loop'))
- grad_down: float32 [4, 4096, 768], P('expert', 'dp', 'loop')
Inputs may be any that keep to these rules, and one draw needn't show every extreme that they name: counts[s, e] is how many of the 4 slots of device s for owner e hold rows, filled from slot 0; in each group of 8 consecutive devices one owner, drawn anew, receives 4 rows from every device, and every other owner at most 2 from each device.
All inputs are finite; a program needn't handle non-finite values.
Results may differ from a plain program's by a relative error of at most 0.0095.
Values may be sent and summed in bfloat16 or wider, within the bound.
No kernel may reach another device: no remote copies, remote signals or barrier semaphores. Data moves between devices by JAX's collectives and lax.ppermute only.
A program may use at most 64 MiB of HBM per device.

v0:
```python
import jax
import jax.numpy as jnp
from jax import lax
from jax.sharding import PartitionSpec as P


def local(x_send, cot_send, counts, w_gate, w_up, w_down):
    owner_count = counts.shape[1]
    capacity = x_send.shape[0] // owner_count
    live_slot = (jnp.arange(capacity, dtype=jnp.int32)[None, :] < counts[0][:, None]).reshape(
        owner_count * capacity, 1
    )
    zero_value = jnp.zeros((), jnp.bfloat16)
    inputs = jnp.where(live_slot, x_send, zero_value)
    cotans = jnp.where(live_slot, cot_send, zero_value)
    arrived, arrived_cot = (
        lax.all_to_all(inputs, "expert", split_axis=0, concat_axis=0, tiled=True),
        lax.all_to_all(cotans, "expert", split_axis=0, concat_axis=0, tiled=True),
    )
    gathered, gathered_cot = (
        lax.all_gather(arrived, "loop", axis=0, tiled=True),
        lax.all_gather(arrived_cot, "loop", axis=0, tiled=True),
    )
    gate_local = w_gate[0]
    up_local = w_up[0]
    down_local = w_down[0]
    gate_pre = jnp.dot(gathered, gate_local, preferred_element_type=jnp.float32)
    up_proj = jnp.dot(gathered, up_local, preferred_element_type=jnp.float32)
    sigmoid_gate = jax.nn.sigmoid(gate_pre)
    active = gate_pre * sigmoid_gate
    hidden = (active * up_proj).astype(jnp.bfloat16)
    grad_hidden = jnp.dot(gathered_cot, down_local, preferred_element_type=jnp.float32)
    grad_gate = (
        grad_hidden * up_proj * sigmoid_gate * (1.0 + gate_pre * (1.0 - sigmoid_gate))
    ).astype(jnp.bfloat16)
    grad_upp = (grad_hidden * active).astype(jnp.bfloat16)
    contract_last = (((1,), (1,)), ((), ()))
    contract_first = (((0,), (0,)), ((), ()))
    partial_value = lax.dot_general(
        grad_gate, gate_local, contract_last, preferred_element_type=jnp.float32
    )
    partial_value = partial_value + lax.dot_general(
        grad_upp, up_local, contract_last, preferred_element_type=jnp.float32
    )
    summed = lax.psum_scatter(
        lax.optimization_barrier(partial_value.astype(jnp.bfloat16))
        .astype(jnp.float32)
        .astype(jnp.bfloat16),
        "loop",
        scatter_dimension=0,
        tiled=True,
    )
    grad_rows = lax.all_to_all(summed, "expert", split_axis=0, concat_axis=0, tiled=True)
    column_part = lax.all_to_all(gathered_cot, "dp", split_axis=1, concat_axis=0, tiled=True)
    hidden_all = lax.all_gather(hidden, "dp", axis=0, tiled=True)
    result = lax.dot_general(
        column_part, hidden_all, contract_first, preferred_element_type=jnp.float32
    )
    grad_down = result[None]
    return (grad_rows, grad_down)


def solution(mesh):
    in_specs = (
        P(("dp", "expert", "loop"), None),
        P(("dp", "expert", "loop"), None),
        P(("dp", "expert", "loop"), None),
        P("expert", None, "loop"),
        P("expert", None, "loop"),
        P("expert", None, "loop"),
    )
    out_specs = (P(("dp", "expert", "loop"), None), P("expert", "dp", "loop"))
    return jax.shard_map(local, mesh=mesh, in_specs=in_specs, out_specs=out_specs, check_vma=False)
```

profile of v0, /device:TPU:0, one launch (start us, length us, event | category | flops | bytes accessed | tf_op | source)
XLA Modules:
  0.0 81.4 jit_solution(18439740056307525910)
XLA Ops:
  7.2 0.0 copy-start
  7.2 0.9 %iota_compare_fusion = pred[4,4]{1,0:T(4,128)(4,1)S(1)} fusion(s32[4]{0:T(128)} %bitcast.33), kind=kLoop, calls=%fused_computation.21 | loop fusion | flops 16 | bytes 32 | tf_op jit(solution)/shard_map/lt | solution.py:10
  8.1 0.1 lt.26
  8.1 1.1 %broadcast_select_fusion.1 = (bf16[16,4096]{1,0:T(8,128)(2,1)S(1)}, bf16[16,4096]{1,0:T(8,128)(2,1)S(1)}) fusion(bf16[16,4096]{1,0:T(8,128)(2,1)} %param.7, pred[16]{0:T(512)(128)(4,1)S(1)} %lt.26, bf16[16,4096]{1,0:T(8,128)(2,1)} %param.6), kind=kLoop, calls=%fused_computation.14 | loop fusion | flops 131072 | bytes 524304 | tf_op jit(solution)/shard_map/jit(_where)/select_n | solution.py:15
  9.2 0.7 all_to_all.38
  9.9 4.3 %all-to-all-start = ((bf16[4,4,4096]{2,1,0:T(4,128)(2,1)}), bf16[4,4,4096]{2,1,0:T(4,128)(2,1)S(1)}, u32[]{:S(2)}, u32[]{:S(2)}) async-start(bf16[4,4,4096]{2,1,0:T(4,128)(2,1)} %all_to_all.38), calls=%async_computation | async-start | bytes 262144 | tf_op jit(solution)/shard_map/all_to_all | solution.py:18
  14.2 0.7 all_to_all.41
  14.9 3.9 %all-to-all-done = bf16[4,4,4096]{2,1,0:T(4,128)(2,1)S(1)} async-done(((bf16[4,4,4096]{2,1,0:T(4,128)(2,1)}), bf16[4,4,4096]{2,1,0:T(4,128)(2,1)S(1)}, u32[]{:S(2)}, u32[]{:S(2)}) %all-to-all-start) | async-done | bytes 131104 | tf_op jit(solution)/shard_map/all_to_all | solution.py:18
  18.8 4.0 %all-to-all-start.1 = ((bf16[4,4,4096]{2,1,0:T(4,128)(2,1)}), bf16[4,4,4096]{2,1,0:T(4,128)(2,1)}, u32[]{:S(2)}, u32[]{:S(2)}) async-start(bf16[4,4,4096]{2,1,0:T(4,128)(2,1)} %all_to_all.41), calls=%async_computation.1 | async-start | bytes 262144 | tf_op jit(solution)/shard_map/all_to_all | solution.py:17
  22.7 0.0 reduce-scatter.2.cloned.1.call-start
  22.8 6.7 %all_gather.9 = bf16[32,4096]{1,0:T(8,128)(2,1)S(1)} all-gather(bf16[16,4096]{1,0:T(8,128)(2,1)S(1)} %all_to_all.40), channel_id=1, replica_groups=mesh['dp'=4,'expert'=4,'loop'=2] {'loop'}, dimensions={0}, use_global_device_ids=true | all-gather | bytes 393216 | tf_op jit(solution)/shard_map/all_gather | solution.py:22
  29.6 0.0 all-to-all-done.1
  29.6 0.9 %all_to_all.43 = bf16[16,4096]{1,0:T(8,128)(2,1)S(1)} reshape(bf16[4,4,4096]{2,1,0:T(4,128)(2,1)} %all-to-all-done.1) | data formatting | bytes 262144 | tf_op jit(solution)/shard_map/all_to_all | solution.py:17
  30.5 0.0 copy-start.1
  30.5 6.0 %all_gather.10 = bf16[32,4096]{1,0:T(8,128)(2,1)S(1)} all-gather(bf16[16,4096]{1,0:T(8,128)(2,1)S(1)} %all_to_all.43), channel_id=1, replica_groups=mesh['dp'=4,'expert'=4,'loop'=2] {'loop'}, dimensions={0}, use_global_device_ids=true | all-gather | bytes 393216 | tf_op jit(solution)/shard_map/all_gather | solution.py:21
  36.5 2.4 %fusion.8 = f32[32,384]{1,0:T(8,128)S(1)} fusion(bf16[32,4096]{1,0:T(8,128)(2,1)S(1)} %all_gather.9, bf16[1,4096,384]{2,1,0:T(8,128)(2,1)} %param.11), kind=kOutput, calls=%fused_computation.9 | convolution fusion | flops 100663296 | bytes 3457024 | tf_op jit(solution)/shard_map/dot_general | solution.py:32
  39.0 0.0 copy-done.1
  39.0 0.5 fusion.3
  39.5 0.0 copy-done
  39.5 0.6 multiply_convert_fusion
  40.1 1.1 %fusion.1 = f32[32,4096]{1,0:T(8,128)S(1)} fusion(bf16[1,4096,384]{2,1,0:T(8,128)(2,1)S(1)} %copy-done.1, f32[32,384]{1,0:T(8,128)S(1)} %fusion.3, f32[32,384]{1,0:T(8,128)S(1)} %fusion.8, f32[32,384]{1,0:T(8,128)S(1)} %get-tuple-element.5), kind=kOutput, calls=%fused_computation.2 | convolution fusion | flops 100786176 | bytes 3817472 | tf_op jit(solution)/shard_map/dot_general | solution.py:39
  41.2 1.8 %fusion = bf16[32,4096]{1,0:T(8,128)(2,1)} fusion(f32[32,4096]{1,0:T(8,128)S(1)} %fusion.1, bf16[1,4096,384]{2,1,0:T(8,128)(2,1)S(1)} %copy-done, f32[32,384]{1,0:T(8,128)S(1)} %fusion.8, f32[32,384]{1,0:T(8,128)S(1)} %fusion.3), kind=kOutput, calls=%fused_computation.1 | convolution fusion | flops 100999168 | bytes 4030464 | tf_op jit(solution)/shard_map/dot_general | solution.py:42
  42.9 0.0 reduce-scatter.2.cloned.1.call-update
  43.0 0.7 copy.12
  43.7 4.9 %all-to-all-start.3 = ((bf16[32,4,1024]{2,0,1:T(8,128)(2,1)}), bf16[32,4,1024]{2,0,1:T(8,128)(2,1)S(1)}, u32[]{:S(2)}, u32[]{:S(2)}) async-start(bf16[32,4,1024]{2,0,1:T(8,128)(2,1)} %bitcast.31), calls=%async_computation.4 | async-start | bytes 524288 | tf_op jit(solution)/shard_map/all_to_all | solution.py:54
  48.6 15.7 %all_gather.11 = bf16[128,384]{1,0:T(8,128)(2,1)} all-gather(bf16[32,384]{1,0:T(8,128)(2,1)S(1)} %get-tuple-element.4), channel_id=1, replica_groups=mesh['dp'=4,'expert'=4,'loop'=2] {'dp'}, dimensions={0}, use_global_device_ids=true | all-gather | bytes 122880 | tf_op jit(solution)/shard_map/all_gather | solution.py:55
  64.3 0.0 reduce-scatter.2.cloned.1.call-done
  64.3 1.6 %all_to_all.44 = bf16[4,4,4096]{2,1,0:T(4,128)(2,1)} reshape(bf16[16,4096]{1,0:T(8,128)(2,1)} %reduce-scatter.2.cloned.1.call-done) | data formatting | bytes 262144 | tf_op jit(solution)/shard_map/all_to_all | solution.py:53
  66.0 0.0 all-to-all-done.3
  66.0 3.3 %all-to-all-start.2 = ((bf16[4,4,4096]{2,1,0:T(4,128)(2,1)}), bf16[4,4,4096]{2,1,0:T(4,128)(2,1)S(1)}, u32[]{:S(2)}, u32[]{:S(2)}) async-start(bf16[4,4,4096]{2,1,0:T(4,128)(2,1)} %all_to_all.44), calls=%async_computation.3 | async-start | bytes 262144 | tf_op jit(solution)/shard_map/all_to_all | solution.py:53
  69.3 2.4 %convolution_bitcast_fusion = f32[1,1024,384]{2,1,0:T(8,128)} fusion(bf16[128,1024]{1,0:T(8,128)(2,1)S(1)} %bitcast.32, bf16[128,384]{1,0:T(8,128)(2,1)} %all_gather.11), kind=kOutput, calls=%fused_computation.11 | convolution fusion | flops 100663296 | bytes 1933312 | tf_op jit(solution)/shard_map/dot_general | solution.py:56
  71.7 2.1 %all-to-all-done.2 = bf16[4,4,4096]{2,1,0:T(4,128)(2,1)S(1)} async-done(((bf16[4,4,4096]{2,1,0:T(4,128)(2,1)}), bf16[4,4,4096]{2,1,0:T(4,128)(2,1)S(1)}, u32[]{:S(2)}, u32[]{:S(2)}) %all-to-all-start.2) | async-done | bytes 131104 | tf_op jit(solution)/shard_map/all_to_all | solution.py:53
  73.9 0.7 all_to_all.46
  (1 shorter events, 0.0 us)
Async XLA Ops:
  7.2 32.4 %copy-start = (bf16[1,4096,384]{2,1,0:T(8,128)(2,1)S(1)}, bf16[1,4096,384]{2,1,0:T(8,128)(2,1)}, u32[]{:S(2)}) copy-start(bf16[1,4096,384]{2,1,0:T(8,128)(2,1)} %param.10) | copy-start | bytes 9437188
  9.9 8.9 %all-to-all-start = ((bf16[4,4,4096]{2,1,0:T(4,128)(2,1)}), bf16[4,4,4096]{2,1,0:T(4,128)(2,1)S(1)}, u32[]{:S(2)}, u32[]{:S(2)}) async-start(bf16[4,4,4096]{2,1,0:T(4,128)(2,1)} %all_to_all.38), calls=%async_computation | async-start | bytes 262144 | tf_op jit(solution)/shard_map/all_to_all | solution.py:18
  18.8 10.8 %all-to-all-start.1 = ((bf16[4,4,4096]{2,1,0:T(4,128)(2,1)}), bf16[4,4,4096]{2,1,0:T(4,128)(2,1)}, u32[]{:S(2)}, u32[]{:S(2)}) async-start(bf16[4,4,4096]{2,1,0:T(4,128)(2,1)} %all_to_all.41), calls=%async_computation.1 | async-start | bytes 262144 | tf_op jit(solution)/shard_map/all_to_all | solution.py:17
  22.7 41.6 %reduce-scatter.2.cloned.1.call-start = ((), (), s32[]{:S(2)}) async-start(), calls=%async_computation.5 | async-start | bytes 393216 | tf_op jit(solution)/shard_map/reduce_scatter | solution.py:45
  30.5 8.4 %copy-start.1 = (bf16[1,4096,384]{2,1,0:T(8,128)(2,1)S(1)}, bf16[1,4096,384]{2,1,0:T(8,128)(2,1)}, u32[]{:S(2)}) copy-start(bf16[1,4096,384]{2,1,0:T(8,128)(2,1)} %param.9) | copy-start | bytes 9437188
  43.7 22.3 %all-to-all-start.3 = ((bf16[32,4,1024]{2,0,1:T(8,128)(2,1)}), bf16[32,4,1024]{2,0,1:T(8,128)(2,1)S(1)}, u32[]{:S(2)}, u32[]{:S(2)}) async-start(bf16[32,4,1024]{2,0,1:T(8,128)(2,1)} %bitcast.31), calls=%async_computation.4 | async-start | bytes 524288 | tf_op jit(solution)/shard_map/all_to_all | solution.py:54
  66.0 7.9 %all-to-all-start.2 = ((bf16[4,4,4096]{2,1,0:T(4,128)(2,1)}), bf16[4,4,4096]{2,1,0:T(4,128)(2,1)S(1)}, u32[]{:S(2)}, u32[]{:S(2)}) async-start(bf16[4,4,4096]{2,1,0:T(4,128)(2,1)} %all_to_all.44), calls=%async_computation.3 | async-start | bytes 262144 | tf_op jit(solution)/shard_map/all_to_all | solution.py:53
Sparse Core Ops, SparseCore 0:
  43.1 13.1 reduce-scatter.1
where the time goes:
time: 82 us; the launch traced here: 81.4 us
  blocking collectives  28.5 us (35%)
  starting transfers between devices  16.5 us (20%)
  between operations  14.1 us (17%)
  matrix products  8.8 us (11%)
  waiting for transfers between devices  6.05 us (7%)
  local copies, waits for them, and re-layouts  5.53 us (7%)
  other arithmetic  1.94 us (2%)
    all_gather x1, blocking collectives, local(): hidden_all = lax.all_gather(hidden, 'dp', axis=0, tiled=True)  15.7 us
    all_gather x1, blocking collectives, local(): lax.all_gather(arrived_cot, 'loop', axis=0, tiled=True)  6.73 us
    all_gather x1, blocking collectives, local(): lax.all_gather(arrived, 'loop', axis=0, tiled=True)  6 us
    all_to_all x1, starting transfers between devices, local(): lax.all_to_all(gathered_cot, 'dp', split_axis=1, concat_axis=0, tiled=True)  4.9 us
    all_to_all x1, starting transfers between devices, local(): lax.all_to_all(cotans, 'expert', split_axis=0, concat_axis=0, tiled=True)  4.26 us
    all_to_all x1, starting transfers between devices, local(): lax.all_to_all(inputs, 'expert', split_axis=0, concat_axis=0, tiled=True)  3.95 us
    all_to_all x1, waiting for transfers between devices, local(): lax.all_to_all(cotans, 'expert', split_axis=0, concat_axis=0, tiled=True)  3.89 us
    all_to_all x1, starting transfers between devices, local(): lax.all_to_all(summed, 'expert', split_axis=0, concat_axis=0, tiled=True)  3.33 us
  transfers between devices with their start and end apart: 5, of which 2 were waited for; matrix products, arithmetic and copies ran while one was open for 4% of the time, Pallas kernels for 0%

commit v1 on v0

--- a/solution.py
+++ b/solution.py
@@ -2,6 +2,28 @@
 import jax.numpy as jnp
 from jax import lax
 from jax.sharding import PartitionSpec as P
+
+
+def in_blocks(x, dim, size):
+    before, after = (x.shape[:dim], x.shape[dim + 1 :])
+    return jnp.moveaxis(x.reshape(*before, size, -1, *after), dim, 0)
+
+
+def laid_out(blocks, dim):
+    blocks = jnp.moveaxis(blocks, 0, dim)
+    shape = blocks.shape
+    return blocks.reshape(*shape[:dim], shape[dim] * shape[dim + 1], *shape[dim + 2 :])
+
+
+def sent_to_each(x, axis, split_dim, concat_dim):
+    size, index = (lax.axis_size(axis), lax.axis_index(axis))
+    blocks = in_blocks(x, split_dim, size)
+    outs = [blocks[index]]
+    for step in range(1, size):
+        sent = blocks[(index + step) % size]
+        outs.append(lax.ppermute(sent, axis, [(i, (i + step) % size) for i in range(size)]))
+    blocks = jnp.stack(outs)[(index - jnp.arange(size)) % size]
+    return laid_out(blocks, concat_dim)
 
 
 def local(x_send, cot_send, counts, w_gate, w_up, w_down):
@@ -15,7 +37,7 @@
     cotans = jnp.where(live_slot, cot_send, zero_value)
     arrived, arrived_cot = (
         lax.all_to_all(inputs, "expert", split_axis=0, concat_axis=0, tiled=True),
-        lax.all_to_all(cotans, "expert", split_axis=0, concat_axis=0, tiled=True),
+        sent_to_each(cotans, "expert", 0, 0),
     )
     gathered, gathered_cot = (
         lax.all_gather(arrived, "loop", axis=0, tiled=True),

time: 82 us -> 80.7 us (0.984)
  waiting for transfers between devices: 6.05 us -> 2.17 us
  matrix products: 8.8 us -> 11.5 us
  starting transfers between devices: 16.5 us -> 15.5 us
    all_to_all x1 -> x0, starting transfers between devices: 4.26 us -> none  [local(): lax.all_to_all(cotans, 'expert', split_axis=0, concat_axis=0, tiled=True)]
    all_to_all x1 -> x0, waiting for transfers between devices: 3.89 us -> none  [local(): lax.all_to_all(cotans, 'expert', split_axis=0, concat_axis=0, tiled=True)]
    ppermute x0 -> x3, starting transfers between devices: none -> 3.28 us  [sent_to_each(): lax.ppermute(sent, axis, [(i, (i + step) % size) for i in range(size)])]
    dot_general x1, matrix products: 0.55 us -> 2.58 us  [local(): gate_pre = jnp.dot(gathered, gate_local, preferred_element_type=jnp.float32)]
  transfers between devices with their start and end apart: 5 -> 7, of which waited for: 2 -> 1; matrix products, arithmetic and copies ran while one was open for 4% -> 9% of each run, Pallas kernels for 0% -> 0%
where the time goes in v1:
time: 80.7 us; the launch traced here: 80.2 us
  blocking collectives  29.2 us (36%)
  starting transfers between devices  15.5 us (19%)
  between operations  14.2 us (18%)
  matrix products  11.5 us (14%)
  local copies, waits for them, and re-layouts  5.6 us (7%)
  waiting for transfers between devices  2.17 us (3%)
  other arithmetic  2.07 us (3%)
    all_gather x1, blocking collectives, local(): hidden_all = lax.all_gather(hidden, 'dp', axis=0, tiled=True)  16.3 us
    all_gather x1, blocking collectives, local(): lax.all_gather(arrived_cot, 'loop', axis=0, tiled=True)  6.67 us
    all_gather x1, blocking collectives, local(): lax.all_gather(arrived, 'loop', axis=0, tiled=True)  6.26 us
    all_to_all x1, starting transfers between devices, local(): lax.all_to_all(gathered_cot, 'dp', split_axis=1, concat_axis=0, tiled=True)  4.87 us
    all_to_all x1, starting transfers between devices, local(): lax.all_to_all(inputs, 'expert', split_axis=0, concat_axis=0, tiled=True)  3.94 us
    all_to_all x1, starting transfers between devices, local(): lax.all_to_all(summed, 'expert', split_axis=0, concat_axis=0, tiled=True)  3.33 us
    ppermute x3, starting transfers between devices, sent_to_each(): lax.ppermute(sent, axis, [(i, (i + step) % size) for i in range(size)])  3.28 us
    dot_general x1, matrix products, local(): jnp.dot(gathered_cot, down_local, preferred_element_type=jnp.float32)  3.06 us
  transfers between devices with their start and end apart: 7, of which 1 were waited for; matrix products, arithmetic and copies ran while one was open for 9% of the time, Pallas kernels for 0%

profile of v1, /device:TPU:0, one launch (start us, length us, event | category | flops | bytes accessed | tf_op | source)
XLA Modules:
  0.0 80.2 jit_solution(14535884734257212106)
XLA Ops:
  7.2 0.0 copy-start
  7.2 0.9 %iota_compare_fusion = pred[4,4]{1,0:T(4,128)(4,1)S(1)} fusion(s32[4]{0:T(128)} %bitcast.47), kind=kLoop, calls=%fused_computation.30 | loop fusion | flops 16 | bytes 32 | tf_op jit(solution)/shard_map/lt | solution.py:32
  8.1 0.1 lt.68
  8.2 1.1 %broadcast_select_fusion.1 = (bf16[16,4096]{1,0:T(8,128)(2,1)S(1)}, bf16[16,4096]{1,0:T(8,128)(2,1)S(1)}) fusion(bf16[16,4096]{1,0:T(8,128)(2,1)} %param.7, pred[16]{0:T(512)(128)(4,1)S(1)} %lt.68, bf16[16,4096]{1,0:T(8,128)(2,1)} %param.6), kind=kLoop, calls=%fused_computation.16 | loop fusion | flops 131072 | bytes 524304 | tf_op jit(solution)/shard_map/jit(_where)/select_n | solution.py:37
  9.3 0.1 reshape.82
  9.3 0.1 constant_dynamic-slice_fusion
  9.4 2.5 %collective-permute-start.2 = (bf16[4,4096]{1,0:T(4,128)(2,1)S(1)}, bf16[4,4096]{1,0:T(4,128)(2,1)S(1)}, u32[]{:S(2)}, u32[]{:S(2)}) collective-permute-start(bf16[4,4096]{1,0:T(4,128)(2,1)S(1)} %get-tuple-element.3), channel_id=1, source_target_pairs={{0,6},{2,0},{4,2},{6,4},{1,7},{3,1},{5,3},{7,5},{8,14},{10,8},{12,... | collective-permute-start | bytes 98312 | tf_op jit(solution)/shard_map/ppermute | solution.py:24
  11.9 0.6 collective-permute-start.1
  12.5 0.2 collective-permute-start
  12.7 0.7 all_to_all.30
  13.4 3.9 %all-to-all-start = ((bf16[4,4,4096]{2,1,0:T(4,128)(2,1)}), bf16[4,4,4096]{2,1,0:T(4,128)(2,1)}, u32[]{:S(2)}, u32[]{:S(2)}) async-start(bf16[4,4,4096]{2,1,0:T(4,128)(2,1)} %all_to_all.30), calls=%async_computation | async-start | bytes 262144 | tf_op jit(solution)/shard_map/all_to_all | solution.py:39
  17.3 0.0 reduce-scatter.2.cloned.1.call-start
  17.4 0.0 collective-permute-done.2
  17.4 0.0 collective-permute-done.1
  17.4 0.0 collective-permute-done
  17.4 0.1 pad_maximum_fusion
  17.6 0.7 gather_fusion
  18.3 6.7 %all_gather.9 = bf16[32,4096]{1,0:T(8,128)(2,1)S(1)} all-gather(bf16[16,4096]{1,0:T(8,128)(2,1)S(1)} %reshape.83), channel_id=1, replica_groups=mesh['dp'=4,'expert'=4,'loop'=2] {'loop'}, dimensions={0}, use_global_device_ids=true | all-gather | bytes 393216 | tf_op jit(solution)/shard_map/all_gather | solution.py:44
  24.9 3.1 %fusion.8 = f32[32,384]{1,0:T(8,128)} fusion(bf16[32,4096]{1,0:T(8,128)(2,1)S(1)} %all_gather.9, bf16[1,4096,384]{2,1,0:T(8,128)(2,1)} %param.11), kind=kOutput, calls=%fused_computation.10 | convolution fusion | flops 100663296 | bytes 3457024 | tf_op jit(solution)/shard_map/dot_general | solution.py:54
  28.0 0.0 all-to-all-done
  28.0 0.9 %all_to_all.32 = bf16[16,4096]{1,0:T(8,128)(2,1)S(1)} reshape(bf16[4,4,4096]{2,1,0:T(4,128)(2,1)} %all-to-all-done) | data formatting | bytes 262144 | tf_op jit(solution)/shard_map/all_to_all | solution.py:39
  28.9 6.3 %all_gather.10 = bf16[32,4096]{1,0:T(8,128)(2,1)S(1)} all-gather(bf16[16,4096]{1,0:T(8,128)(2,1)S(1)} %all_to_all.32), channel_id=1, replica_groups=mesh['dp'=4,'expert'=4,'loop'=2] {'loop'}, dimensions={0}, use_global_device_ids=true | all-gather | bytes 393216 | tf_op jit(solution)/shard_map/all_gather | solution.py:43
  35.2 0.0 copy-start.1
  35.2 0.0 copy-start.2
  35.2 2.6 %fusion.3 = f32[32,384]{1,0:T(8,128)S(1)} fusion(bf16[32,4096]{1,0:T(8,128)(2,1)S(1)} %all_gather.10, bf16[1,4096,384]{2,1,0:T(8,128)(2,1)} %param.9), kind=kOutput, calls=%fused_computation.5 | convolution fusion | flops 100663296 | bytes 3457024 | tf_op jit(solution)/shard_map/dot_general | solution.py:49
  37.8 0.0 copy-done
  37.8 0.6 multiply_convert_fusion
  38.4 0.0 copy-done.1
  38.4 0.0 copy-done.2
  38.4 1.1 %fusion.1 = f32[32,4096]{1,0:T(8,128)S(1)} fusion(bf16[1,4096,384]{2,1,0:T(8,128)(2,1)S(1)} %copy-done.1, f32[32,384]{1,0:T(8,128)S(1)} %fusion.3, f32[32,384]{1,0:T(8,128)S(1)} %copy-done.2, f32[32,384]{1,0:T(8,128)S(1)} %get-tuple-element.9), kind=kOutput, calls=%fused_computation.3 | convolution fusion | flops 100786176 | bytes 3817472 | tf_op jit(solution)/shard_map/dot_general | solution.py:61
  39.4 1.8 %fusion = bf16[32,4096]{1,0:T(8,128)(2,1)} fusion(f32[32,4096]{1,0:T(8,128)S(1)} %fusion.1, bf16[1,4096,384]{2,1,0:T(8,128)(2,1)S(1)} %copy-done, f32[32,384]{1,0:T(8,128)S(1)} %copy-done.2, f32[32,384]{1,0:T(8,128)S(1)} %fusion.3), kind=kOutput, calls=%fused_computation.2 | convolution fusion | flops 100999168 | bytes 4030464 | tf_op jit(solution)/shard_map/dot_general | solution.py:64
  41.2 0.0 reduce-scatter.2.cloned.1.call-update
  41.3 0.7 copy.12
  42.0 4.9 %all-to-all-start.2 = ((bf16[32,4,1024]{2,0,1:T(8,128)(2,1)}), bf16[32,4,1024]{2,0,1:T(8,128)(2,1)S(1)}, u32[]{:S(2)}, u32[]{:S(2)}) async-start(bf16[32,4,1024]{2,0,1:T(8,128)(2,1)} %bitcast.42), calls=%async_computation.3 | async-start | bytes 524288 | tf_op jit(solution)/shard_map/all_to_all | solution.py:76
  46.8 16.3 %all_gather.11 = bf16[128,384]{1,0:T(8,128)(2,1)} all-gather(bf16[32,384]{1,0:T(8,128)(2,1)S(1)} %get-tuple-element.8), channel_id=1, replica_groups=mesh['dp'=4,'expert'=4,'loop'=2] {'dp'}, dimensions={0}, use_global_device_ids=true | all-gather | bytes 122880 | tf_op jit(solution)/shard_map/all_gather | solution.py:77
  63.1 0.0 reduce-scatter.2.cloned.1.call-done
  63.1 1.6 %all_to_all.33 = bf16[4,4,4096]{2,1,0:T(4,128)(2,1)} reshape(bf16[16,4096]{1,0:T(8,128)(2,1)} %reduce-scatter.2.cloned.1.call-done) | data formatting | bytes 262144 | tf_op jit(solution)/shard_map/all_to_all | solution.py:75
  64.8 0.0 all-to-all-done.2
  64.8 3.3 %all-to-all-start.1 = ((bf16[4,4,4096]{2,1,0:T(4,128)(2,1)}), bf16[4,4,4096]{2,1,0:T(4,128)(2,1)S(1)}, u32[]{:S(2)}, u32[]{:S(2)}) async-start(bf16[4,4,4096]{2,1,0:T(4,128)(2,1)} %all_to_all.33), calls=%async_computation.2 | async-start | bytes 262144 | tf_op jit(solution)/shard_map/all_to_all | solution.py:75
  68.1 2.4 %convolution_bitcast_fusion = f32[1,1024,384]{2,1,0:T(8,128)} fusion(bf16[128,1024]{1,0:T(8,128)(2,1)S(1)} %bitcast.43, bf16[128,384]{1,0:T(8,128)(2,1)} %all_gather.11), kind=kOutput, calls=%fused_computation.12 | convolution fusion | flops 100663296 | bytes 1933312 | tf_op jit(solution)/shard_map/dot_general | solution.py:78
  70.5 2.1 %all-to-all-done.1 = bf16[4,4,4096]{2,1,0:T(4,128)(2,1)S(1)} async-done(((bf16[4,4,4096]{2,1,0:T(4,128)(2,1)}), bf16[4,4,4096]{2,1,0:T(4,128)(2,1)S(1)}, u32[]{:S(2)}, u32[]{:S(2)}) %all-to-all-start.1) | async-done | bytes 131104 | tf_op jit(solution)/shard_map/all_to_all | solution.py:75
  72.7 0.7 all_to_all.35
  (3 shorter events, 0.1 us)
Async XLA Ops:
  7.2 30.6 %copy-start = (bf16[1,4096,384]{2,1,0:T(8,128)(2,1)S(1)}, bf16[1,4096,384]{2,1,0:T(8,128)(2,1)}, u32[]{:S(2)}) copy-start(bf16[1,4096,384]{2,1,0:T(8,128)(2,1)} %param.10) | copy-start | bytes 9437188
  9.4 8.0 %collective-permute-start.2 = (bf16[4,4096]{1,0:T(4,128)(2,1)S(1)}, bf16[4,4096]{1,0:T(4,128)(2,1)S(1)}, u32[]{:S(2)}, u32[]{:S(2)}) collective-permute-start(bf16[4,4096]{1,0:T(4,128)(2,1)S(1)} %get-tuple-element.3), channel_id=1, source_target_pairs={{0,6},{2,0},{4,2},{6,4},{1,7},{3,1},{5,3},{7,5},{8,14},{10,8},{12,... | collective-permute-start | bytes 98312 | tf_op jit(solution)/shard_map/ppermute | solution.py:24
  11.9 5.5 %collective-permute-start.1 = (bf16[4,4096]{1,0:T(4,128)(2,1)S(1)}, bf16[4,4096]{1,0:T(4,128)(2,1)S(1)}, u32[]{:S(2)}, u32[]{:S(2)}) collective-permute-start(bf16[4,4096]{1,0:T(4,128)(2,1)S(1)} %get-tuple-element.4), channel_id=1, source_target_pairs={{0,4},{2,6},{4,0},{6,2},{1,5},{3,7},{5,1},{7,3},{8,12},{10,14},{12... | collective-permute-start | bytes 98312 | tf_op jit(solution)/shard_map/ppermute | solution.py:24
  12.5 4.9 %collective-permute-start = (bf16[4,4096]{1,0:T(4,128)(2,1)S(1)}, bf16[4,4096]{1,0:T(4,128)(2,1)S(1)}, u32[]{:S(2)}, u32[]{:S(2)}) collective-permute-start(bf16[4,4096]{1,0:T(4,128)(2,1)S(1)} %get-tuple-element.5), channel_id=1, source_target_pairs={{0,2},{2,4},{4,6},{6,0},{1,3},{3,5},{5,7},{7,1},{8,10},{10,12},{12... | collective-permute-start | bytes 98312 | tf_op jit(solution)/shard_map/ppermute | solution.py:24
  13.4 14.6 %all-to-all-start = ((bf16[4,4,4096]{2,1,0:T(4,128)(2,1)}), bf16[4,4,4096]{2,1,0:T(4,128)(2,1)}, u32[]{:S(2)}, u32[]{:S(2)}) async-start(bf16[4,4,4096]{2,1,0:T(4,128)(2,1)} %all_to_all.30), calls=%async_computation | async-start | bytes 262144 | tf_op jit(solution)/shard_map/all_to_all | solution.py:39
  17.3 45.8 %reduce-scatter.2.cloned.1.call-start = ((), (), s32[]{:S(2)}) async-start(), calls=%async_computation.4 | async-start | bytes 393216 | tf_op jit(solution)/shard_map/reduce_scatter | solution.py:67
  35.2 3.2 %copy-start.1 = (bf16[1,4096,384]{2,1,0:T(8,128)(2,1)S(1)}, bf16[1,4096,384]{2,1,0:T(8,128)(2,1)}, u32[]{:S(2)}) copy-start(bf16[1,4096,384]{2,1,0:T(8,128)(2,1)} %param.9) | copy-start | bytes 9437188
  35.2 3.2 %copy-start.2 = (f32[32,384]{1,0:T(8,128)S(1)}, f32[32,384]{1,0:T(8,128)}, u32[]{:S(2)}) copy-start(f32[32,384]{1,0:T(8,128)} %fusion.8) | copy-start | bytes 147460
  42.0 22.8 %all-to-all-start.2 = ((bf16[32,4,1024]{2,0,1:T(8,128)(2,1)}), bf16[32,4,1024]{2,0,1:T(8,128)(2,1)S(1)}, u32[]{:S(2)}, u32[]{:S(2)}) async-start(bf16[32,4,1024]{2,0,1:T(8,128)(2,1)} %bitcast.42), calls=%async_computation.3 | async-start | bytes 524288 | tf_op jit(solution)/shard_map/all_to_all | solution.py:76
  64.8 7.9 %all-to-all-start.1 = ((bf16[4,4,4096]{2,1,0:T(4,128)(2,1)}), bf16[4,4,4096]{2,1,0:T(4,128)(2,1)S(1)}, u32[]{:S(2)}, u32[]{:S(2)}) async-start(bf16[4,4,4096]{2,1,0:T(4,128)(2,1)} %all_to_all.33), calls=%async_computation.2 | async-start | bytes 262144 | tf_op jit(solution)/shard_map/all_to_all | solution.py:75
Sparse Core Ops, SparseCore 0:
  41.4 12.2 reduce-scatter.1
